TPU v7x, 512 devices: a whole 4x4x16 slice. The times are simulated.
512 devices in a mesh: seq: 128 (over y, z, core), head: 4 (over x).
Axes of the slice: x: 4, y: 4, z: 16, core: 2. Of those that a mesh axis runs over, the one named last changes fastest.
Arguments:
- queries: bfloat16 [65536, 2048], P('seq', 'head'), may hold values from -6 to 6
- key_vectors: bfloat16 [65536, 2048], P('seq', 'head'), may hold values from -6 to 6
- values: bfloat16 [65536, 2048], P('seq', 'head'), may hold values from -6 to 6
- out_weight: bfloat16 [2048, 2048], P('head', 'seq'), may hold values from -4 to 4
Outputs:
- mixed: bfloat16 [65536, 2048], P('seq', 'head')
All inputs are finite; a program needn't handle non-finite values.
Results may differ from a plain program's by a relative error of at most 0.0095.
Values may be sent and summed in bfloat16 or wider, within the bound.
No kernel may reach another device: no remote copies, remote signals or barrier semaphores. Data moves between devices by JAX's collectives and lax.ppermute only.
A program may use at most 64 MiB of HBM per device.

v0:
```python
import math
import jax
import jax.numpy as jnp
from jax import lax
from jax.sharding import PartitionSpec as P

HEAD_DIM = 128
BLOCK = 128
LEVELS = 5


def partner(value, axis, stride):
    mask = 2**stride
    pairs = [(source, source ^ mask) for source in range(lax.axis_size(axis))]
    return lax.ppermute(value, axis, pairs)


def pool_mean(array_in):
    paired = array_in.astype(jnp.float32).reshape(array_in.shape[0] // 2, 2, array_in.shape[1])
    return ((paired[:, 0] + paired[:, 1]) * 0.5).astype(jnp.bfloat16)


def pool_sum(array_in):
    paired = array_in.astype(jnp.float32).reshape(array_in.shape[0] // 2, 2, array_in.shape[1])
    return (paired[:, 0] + paired[:, 1]).astype(jnp.bfloat16)


def to_blocks(array_in, head_count, block_rows):
    return array_in.reshape(-1, block_rows, head_count, array_in.shape[1] // head_count)


def swap_pairs(blocked):
    block_count = blocked.shape[0]
    return blocked.reshape((block_count // 2, 2) + blocked.shape[1:])[:, ::-1].reshape(
        blocked.shape
    )


def level_terms(
    blocked_query_rows, blocked_key_rows, blocked_value_rows, weight, logit_scale_factor
):
    attention_logits = (
        jnp.einsum(
            "bqhd,bkhd->bhqk",
            blocked_query_rows,
            blocked_key_rows,
            preferred_element_type=jnp.float32,
        )
        * logit_scale_factor
    )
    peak_score = jnp.max(attention_logits, axis=-1)
    expo = jnp.exp(attention_logits - peak_score[..., None])
    mass = weight * jnp.sum(expo, axis=-1)
    weighted_value_sum = jnp.einsum(
        "bhqk,bkhd->bqhd",
        expo.astype(jnp.bfloat16),
        blocked_value_rows,
        preferred_element_type=jnp.float32,
    )
    head_count = blocked_query_rows.shape[2]
    peak_rows = jnp.transpose(peak_score, (0, 2, 1)).reshape(-1, head_count)
    mass_rows = jnp.transpose(mass, (0, 2, 1)).reshape(-1, head_count)
    return (
        peak_rows,
        mass_rows,
        weighted_value_sum.reshape(-1, head_count, weighted_value_sum.shape[3]),
    )


def merge_level(running, terms, factor):
    running_max, running_sum, running_out = running
    peak_rows = jnp.repeat(terms[0], factor, axis=0)
    mass_rows = jnp.repeat(terms[1], factor, axis=0)
    weighted_value_sum = jnp.repeat(terms[2], factor, axis=0)
    newest = jnp.maximum(running_max, peak_rows)
    keep_old = jnp.exp(running_max - newest)
    keep_new = jnp.exp(peak_rows - newest)
    return (
        newest,
        running_sum * keep_old + mass_rows * keep_new,
        running_out * keep_old[..., None] + weighted_value_sum * keep_new[..., None],
    )


def body(queries, key_vectors, values, out_weight):
    row_count, col_count = queries.shape
    head_count = col_count // HEAD_DIM
    logit_scale_factor = 1.0 / math.sqrt(HEAD_DIM)
    seq_index = lax.axis_index("seq")
    blocked_key_rows = to_blocks(key_vectors, head_count, BLOCK)
    blocked_value_rows = to_blocks(values, head_count, BLOCK)
    near_keys = jnp.concatenate([blocked_key_rows, swap_pairs(blocked_key_rows)], axis=1)
    near_values = jnp.concatenate([blocked_value_rows, swap_pairs(blocked_value_rows)], axis=1)
    running = level_terms(
        to_blocks(queries, head_count, BLOCK), near_keys, near_values, 1.0, logit_scale_factor
    )
    level_queries, level_keys, level_values = (queries, key_vectors, values)
    far_keys, far_values = (key_vectors, values)
    is_local = True
    partner_bit = 0
    for coarse_level in range(1, LEVELS + 1):
        level_queries = pool_mean(level_queries)
        if is_local:
            level_keys = pool_mean(level_keys)
            level_values = pool_sum(level_values)
            is_local = level_keys.shape[0] >= 2 * BLOCK
        else:
            leading = seq_index >> partner_bit - 1 & 1 == 0
            level_keys = pool_mean(
                jnp.concatenate(
                    [
                        jnp.where(leading, level_keys, far_keys),
                        jnp.where(leading, far_keys, level_keys),
                    ],
                    axis=0,
                )
            )
            level_values = pool_sum(
                jnp.concatenate(
                    [
                        jnp.where(leading, level_values, far_values),
                        jnp.where(leading, far_values, level_values),
                    ],
                    axis=0,
                )
            )
        if is_local:
            blocked_key_rows = swap_pairs(to_blocks(level_keys, head_count, BLOCK))
            blocked_value_rows = swap_pairs(to_blocks(level_values, head_count, BLOCK))
        else:
            far_keys, far_values = partner((level_keys, level_values), "seq", partner_bit)
            partner_bit += 1
            blocked_key_rows = to_blocks(far_keys, head_count, BLOCK)
            blocked_value_rows = to_blocks(far_values, head_count, BLOCK)
        blocked_query_rows = to_blocks(
            level_queries, head_count, level_queries.shape[0] // blocked_key_rows.shape[0]
        )
        terms = level_terms(
            blocked_query_rows,
            blocked_key_rows,
            blocked_value_rows,
            2.0**coarse_level,
            logit_scale_factor,
        )
        running = merge_level(running, terms, 2**coarse_level)
    attended = (
        (running[2] / running[1][..., None]).reshape(row_count, col_count).astype(jnp.bfloat16)
    )
    partial_terms = jnp.dot(
        attended,
        lax.all_gather(out_weight, "seq", axis=1, tiled=True),
        preferred_element_type=jnp.float32,
    )
    rounded_terms = partial_terms.astype(jnp.bfloat16).astype(jnp.float32)
    mixed = lax.psum_scatter(
        rounded_terms.astype(jnp.bfloat16), "head", scatter_dimension=1, tiled=True
    )
    return mixed


def solution(mesh):
    in_specs = (P("seq", "head"), P("seq", "head"), P("seq", "head"), P("head", "seq"))
    out_specs = P("seq", "head")
    return jax.shard_map(body, mesh=mesh, in_specs=in_specs, out_specs=out_specs, check_vma=False)
```

profile of v0, /device:TPU:1, one launch (start us, length us, event | category | flops | bytes accessed | tf_op | source)
XLA Modules:
  0.0 223.5 jit_solution(2739491692825542733)
XLA Ops:
  7.3 1.7 reshape.785
  10.7 8.7 %collective-permute-start = (bf16[128,512]{1,0:T(8,128)(2,1)S(1)}, bf16[128,512]{1,0:T(8,128)(2,1)}, u32[]{:S(2)}, u32[]{:S(2)}) collective-permute-start(bf16[128,512]{1,0:T(8,128)(2,1)S(1)} %fusion.53), channel_id=1, source_target_pairs={{0,4},{4,0},{8,12},{12,8},{16,20},{20,16},{24,28},{28,24},{32,36},... | collective-permute-start | bytes 393224 | tf_op jit(solution)/shard_map/ppermute | solution.py:15
  22.6 2.2 collective-permute-start.1
  33.2 1.0 copy.283
  35.3 1.1 convert_reduce_fusion.1
  39.2 1.0 fusion.1
  43.9 1.0 copy.311
  47.0 1.0 copy.317
  48.4 1.7 broadcast_select_fusion.9
  51.0 1.9 collective-permute-start.3
  52.9 1.0 maximum_convert_fusion
  54.6 3.6 %collective-permute-start.2 = (bf16[128,512]{1,0:T(8,128)(2,1)S(1)}, bf16[128,512]{1,0:T(8,128)(2,1)}, u32[]{:S(2)}, u32[]{:S(2)}) collective-permute-start(bf16[128,512]{1,0:T(8,128)(2,1)S(1)} %fusion.54), channel_id=1, source_target_pairs={{0,8},{4,12},{8,0},{12,4},{16,24},{20,28},{24,16},{28,20},{32,40},... | collective-permute-start | bytes 393224 | tf_op jit(solution)/shard_map/ppermute | solution.py:15
  59.1 1.9 collective-permute-start.5
  61.3 1.0 copy.323
  62.3 1.1 fusion.115
  67.5 4.0 %collective-permute-start.4 = (bf16[128,512]{1,0:T(8,128)(2,1)S(1)}, bf16[128,512]{1,0:T(8,128)(2,1)}, u32[]{:S(2)}, u32[]{:S(2)}) collective-permute-start(bf16[128,512]{1,0:T(8,128)(2,1)S(1)} %fusion.55), channel_id=1, source_target_pairs={{0,16},{4,20},{8,24},{12,28},{16,0},{20,4},{24,8},{28,12},{32,48},... | collective-permute-start | bytes 393224 | tf_op jit(solution)/shard_map/ppermute | solution.py:15
  71.5 1.3 fusion.99
  75.1 5.7 %collective-permute-start.7 = (bf16[128,512]{1,0:T(8,128)(2,1)}, bf16[128,512]{1,0:T(8,128)(2,1)}, u32[]{:S(2)}, u32[]{:S(2)}) collective-permute-start(bf16[128,512]{1,0:T(8,128)(2,1)} %bitcast.335), channel_id=1, source_target_pairs={{0,32},{4,36},{8,40},{12,44},{16,48},{20,52},{24,56},{28,60},{32,0... | collective-permute-start | bytes 393224 | tf_op jit(solution)/shard_map/ppermute | solution.py:15
  80.8 1.0 copy.341
  81.8 1.0 copy.335
  82.9 1.0 fusion.114
  87.5 3.5 %collective-permute-start.6 = (bf16[128,512]{1,0:T(8,128)(2,1)S(1)}, bf16[128,512]{1,0:T(8,128)(2,1)S(1)}, u32[]{:S(2)}, u32[]{:S(2)}) collective-permute-start(bf16[128,512]{1,0:T(8,128)(2,1)S(1)} %fusion.56), channel_id=1, source_target_pairs={{0,32},{4,36},{8,40},{12,44},{16,48},{20,52},{24,56},{28,60},{32,0... | collective-permute-start | bytes 393224 | tf_op jit(solution)/shard_map/ppermute | solution.py:15
  91.4 3.5 %collective-permute-done.7 = bf16[128,512]{1,0:T(8,128)(2,1)} collective-permute-done((bf16[128,512]{1,0:T(8,128)(2,1)}, bf16[128,512]{1,0:T(8,128)(2,1)}, u32[]{:S(2)}, u32[]{:S(2)}) %collective-permute-start.7) | collective-permute-done | bytes 131104 | tf_op jit(solution)/shard_map/ppermute | solution.py:15
  94.9 1.0 copy.351
  95.9 11.2 %collective-permute-done.6 = bf16[128,512]{1,0:T(8,128)(2,1)S(1)} collective-permute-done((bf16[128,512]{1,0:T(8,128)(2,1)S(1)}, bf16[128,512]{1,0:T(8,128)(2,1)S(1)}, u32[]{:S(2)}, u32[]{:S(2)}) %collective-permute-start.6) | collective-permute-done | bytes 131104 | tf_op jit(solution)/shard_map/ppermute | solution.py:15
  111.2 1.6 copy.297
  112.8 1.6 copy.314
  114.3 1.6 copy.326
  117.6 53.3 %all-gather.2.cloned.1.call-done = bf16[512,2048]{0,1:T(8,128)(2,1)} async-done(((bf16[512,16]{0,1:T(8,128)(2,1)}), bf16[512,2048]{0,1:T(8,128)(2,1)}) %all-gather.2.cloned.1.call-update) | async-done | bytes 2097168 | tf_op jit(solution)/shard_map/all_gather | solution.py:151
  171.1 1.6 mul.426
  179.8 3.5 %convolution_convert_fusion = bf16[512,2048]{1,0:T(8,128)(2,1)} fusion(bf16[512,2048]{0,1:T(8,128)(2,1)S(1)} %copy-done.2, f32[64,8,4,128]{3,2,1,0:T(4,128)S(1)} %bitcast.346, f32[64,8,4,128]{3,2,1,0:T(4,128)S(1)} %bitcast.341, f32[64,8,4,128]{3,2,1,0:T(4,128)S(1)} %bitcast.351, f32[64,8,4,128]{3,2,1,0:T(4,128)S(1)} %bitcast.336, ...), kind=kOutput, calls=%fused_computation | convolution fusion | flops 1079246848 | bytes 21102592 | tf_op jit(solution)/shard_map/dot_general | solution.py:149
  183.4 33.3 %reduce-scatter.2.cloned.1.call-done = bf16[512,512]{1,0:T(8,128)(2,1)} async-done(((bf16[512,2048]{1,0:T(8,128)(2,1)}), bf16[512,512]{1,0:T(8,128)(2,1)}) %reduce-scatter.2.cloned.1.call-update) | async-done | bytes 524304 | tf_op jit(solution)/shard_map/reduce_scatter | solution.py:155
  (215 shorter events, 49.0 us)
Async XLA Ops:
  6.5 164.4 %all-gather.2.cloned.1.call-start = ((), (), s32[]{:S(2)}) async-start(), calls=%async_computation.1 | async-start | bytes 2113536 | tf_op jit(solution)/shard_map/all_gather | solution.py:151
  7.3 209.4 %reduce-scatter.2.cloned.1.call-start = ((), (), s32[]{:S(2)}) async-start(), calls=%async_computation.2 | async-start | bytes 2621440 | tf_op jit(solution)/shard_map/reduce_scatter | solution.py:155
  9.8 9.7 %copy-start.1 = (bf16[512,512]{1,0:T(8,128)(2,1)S(1)}, bf16[512,512]{1,0:T(8,128)(2,1)}, u32[]{:S(2)}) copy-start(bf16[512,512]{1,0:T(8,128)(2,1)} %param.6) | copy-start | bytes 1572868
  10.7 33.1 %collective-permute-start = (bf16[128,512]{1,0:T(8,128)(2,1)S(1)}, bf16[128,512]{1,0:T(8,128)(2,1)}, u32[]{:S(2)}, u32[]{:S(2)}) collective-permute-start(bf16[128,512]{1,0:T(8,128)(2,1)S(1)} %fusion.53), channel_id=1, source_target_pairs={{0,4},{4,0},{8,12},{12,8},{16,20},{20,16},{24,28},{28,24},{32,36},... | collective-permute-start | bytes 393224 | tf_op jit(solution)/shard_map/ppermute | solution.py:15
  21.0 3.8 %copy-start = (bf16[512,512]{1,0:T(8,128)(2,1)S(1)}, bf16[512,512]{1,0:T(8,128)(2,1)}, u32[]{:S(2)}) copy-start(bf16[512,512]{1,0:T(8,128)(2,1)} %param.5) | copy-start | bytes 1572868
  22.6 4.4 %copy-start.3 = (bf16[512,512]{1,0:T(8,128)(2,1)S(1)}, bf16[512,512]{1,0:T(8,128)(2,1)}, u32[]{:S(2)}) copy-start(bf16[512,512]{1,0:T(8,128)(2,1)} %param.4) | copy-start | bytes 1572868
  22.6 24.5 %collective-permute-start.1 = (bf16[128,512]{1,0:T(8,128)(2,1)}, bf16[128,512]{1,0:T(8,128)(2,1)}, u32[]{:S(2)}, u32[]{:S(2)}) collective-permute-start(bf16[128,512]{1,0:T(8,128)(2,1)} %fusion.50), channel_id=1, source_target_pairs={{0,4},{4,0},{8,12},{12,8},{16,20},{20,16},{24,28},{28,24},{32,36},... | collective-permute-start | bytes 393224 | tf_op jit(solution)/shard_map/ppermute | solution.py:15
  29.3 3.0 %copy-start.4 = (bf16[2,2,128,4,128]{4,3,2,1,0:T(4,128)(2,1)S(1)}, bf16[2,2,128,4,128]{4,3,2,1,0:T(4,128)(2,1)}, u32[]{:S(2)}) copy-start(bf16[2,2,128,4,128]{4,3,2,1,0:T(4,128)(2,1)} %reshape_reshape.9) | copy-start | bytes 1572868
  34.6 3.1 %copy-start.11 = (bf16[1,2,128,4,128]{4,3,2,1,0:T(4,128)(2,1)S(1)}, bf16[1,2,128,4,128]{4,3,2,1,0:T(4,128)(2,1)}, u32[]{:S(2)}) copy-start(bf16[1,2,128,4,128]{4,3,2,1,0:T(4,128)(2,1)} %convert_element_type.246) | copy-start | bytes 786436
  34.6 3.2 %copy-start.12 = (bf16[2,128,4,128]{3,2,1,0:T(4,128)(2,1)S(1)}, bf16[2,128,4,128]{3,2,1,0:T(4,128)(2,1)}, u32[]{:S(2)}) copy-start(bf16[2,128,4,128]{3,2,1,0:T(4,128)(2,1)} %convert_element_type.244) | copy-start | bytes 786436
  51.0 7.3 %collective-permute-start.3 = (bf16[128,512]{1,0:T(8,128)(2,1)S(1)}, bf16[128,512]{1,0:T(8,128)(2,1)S(1)}, u32[]{:S(2)}, u32[]{:S(2)}) collective-permute-start(bf16[128,512]{1,0:T(8,128)(2,1)S(1)} %fusion.51), channel_id=1, source_target_pairs={{0,8},{4,12},{8,0},{12,4},{16,24},{20,28},{24,16},{28,20},{32,40},... | collective-permute-start | bytes 393224 | tf_op jit(solution)/shard_map/ppermute | solution.py:15
  54.6 6.6 %collective-permute-start.2 = (bf16[128,512]{1,0:T(8,128)(2,1)S(1)}, bf16[128,512]{1,0:T(8,128)(2,1)}, u32[]{:S(2)}, u32[]{:S(2)}) collective-permute-start(bf16[128,512]{1,0:T(8,128)(2,1)S(1)} %fusion.54), channel_id=1, source_target_pairs={{0,8},{4,12},{8,0},{12,4},{16,24},{20,28},{24,16},{28,20},{32,40},... | collective-permute-start | bytes 393224 | tf_op jit(solution)/shard_map/ppermute | solution.py:15
  59.1 13.7 %collective-permute-start.5 = (bf16[128,512]{1,0:T(8,128)(2,1)S(1)}, bf16[128,512]{1,0:T(8,128)(2,1)}, u32[]{:S(2)}, u32[]{:S(2)}) collective-permute-start(bf16[128,512]{1,0:T(8,128)(2,1)S(1)} %fusion.52), channel_id=1, source_target_pairs={{0,16},{4,20},{8,24},{12,28},{16,0},{20,4},{24,8},{28,12},{32,48},... | collective-permute-start | bytes 393224 | tf_op jit(solution)/shard_map/ppermute | solution.py:15
  67.5 14.4 %collective-permute-start.4 = (bf16[128,512]{1,0:T(8,128)(2,1)S(1)}, bf16[128,512]{1,0:T(8,128)(2,1)}, u32[]{:S(2)}, u32[]{:S(2)}) collective-permute-start(bf16[128,512]{1,0:T(8,128)(2,1)S(1)} %fusion.55), channel_id=1, source_target_pairs={{0,16},{4,20},{8,24},{12,28},{16,0},{20,4},{24,8},{28,12},{32,48},... | collective-permute-start | bytes 393224 | tf_op jit(solution)/shard_map/ppermute | solution.py:15
  75.1 19.7 %collective-permute-start.7 = (bf16[128,512]{1,0:T(8,128)(2,1)}, bf16[128,512]{1,0:T(8,128)(2,1)}, u32[]{:S(2)}, u32[]{:S(2)}) collective-permute-start(bf16[128,512]{1,0:T(8,128)(2,1)} %bitcast.335), channel_id=1, source_target_pairs={{0,32},{4,36},{8,40},{12,44},{16,48},{20,52},{24,56},{28,60},{32,0... | collective-permute-start | bytes 393224 | tf_op jit(solution)/shard_map/ppermute | solution.py:15
  83.9 2.6 %copy-start.22 = (f32[4,32]{1,0:T(4,128)}, f32[4,32]{1,0:T(4,128)S(1)}, u32[]{:S(2)}) copy-start(f32[4,32]{1,0:T(4,128)S(1)} %get-tuple-element.60) | copy-start | bytes 1540
  86.5 20.7 %copy-start.20 = (bf16[16,512]{1,0:T(8,128)(2,1)S(1)}, bf16[16,512]{1,0:T(8,128)(2,1)}, u32[]{:S(2)}) copy-start(bf16[16,512]{1,0:T(8,128)(2,1)} %convert_reduce_fusion.4) | copy-start | bytes 49156
  86.6 4.4 %copy-start.23 = (f32[4,32]{1,0:T(4,128)S(1)}, f32[4,32]{1,0:T(4,128)}, u32[]{:S(2)}) copy-start(f32[4,32]{1,0:T(4,128)} %copy-done.22) | copy-start | bytes 1540
  86.6 22.2 %copy-start.18 = (f32[512,4]{0,1:T(4,128)S(1)}, f32[512,4]{0,1:T(4,128)}, u32[]{:S(2)}) copy-start(f32[512,4]{0,1:T(4,128)} %reshape.749) | copy-start | bytes 24580
  86.6 22.2 %copy-start.19 = (f32[512,4]{0,1:T(4,128)S(1)}, f32[512,4]{0,1:T(4,128)}, u32[]{:S(2)}) copy-start(f32[512,4]{0,1:T(4,128)} %reshape.755) | copy-start | bytes 24580
  86.6 22.2 %copy-start.21 = (f32[4,4,128]{2,1,0:T(4,128)S(1)}, f32[4,4,128]{2,1,0:T(4,128)}, u32[]{:S(2)}) copy-start(f32[4,4,128]{2,1,0:T(4,128)} %fusion.1) | copy-start | bytes 24580
  86.6 22.2 %copy-start.24 = (f32[512,4]{0,1:T(4,128)S(1)}, f32[512,4]{0,1:T(4,128)}, u32[]{:S(2)}) copy-start(f32[512,4]{0,1:T(4,128)} %copy.356) | copy-start | bytes 24580
  86.6 22.2 %copy-start.25 = (f32[512,4]{0,1:T(4,128)S(1)}, f32[512,4]{0,1:T(4,128)}, u32[]{:S(2)}) copy-start(f32[512,4]{0,1:T(4,128)} %reshape.775) | copy-start | bytes 24580
  87.0 21.9 %copy-start.26 = (f32[512,4]{0,1:T(4,128)S(1)}, f32[512,4]{0,1:T(4,128)}, u32[]{:S(2)}) copy-start(f32[512,4]{0,1:T(4,128)} %reshape.777) | copy-start | bytes 24580
  87.0 21.9 %copy-start.27 = (f32[512,4]{0,1:T(4,128)S(1)}, f32[512,4]{0,1:T(4,128)}, u32[]{:S(2)}) copy-start(f32[512,4]{0,1:T(4,128)} %reshape.761) | copy-start | bytes 24580
  87.0 21.9 %copy-start.30 = (f32[512,4]{0,1:T(4,128)S(1)}, f32[512,4]{0,1:T(4,128)}, u32[]{:S(2)}) copy-start(f32[512,4]{0,1:T(4,128)} %get-tuple-element.18) | copy-start | bytes 24580
  87.0 21.9 %copy-start.31 = (f32[512,4]{0,1:T(4,128)S(1)}, f32[512,4]{0,1:T(4,128)}, u32[]{:S(2)}) copy-start(f32[512,4]{0,1:T(4,128)} %get-tuple-element.19) | copy-start | bytes 24580
  87.5 19.6 %collective-permute-start.6 = (bf16[128,512]{1,0:T(8,128)(2,1)S(1)}, bf16[128,512]{1,0:T(8,128)(2,1)S(1)}, u32[]{:S(2)}, u32[]{:S(2)}) collective-permute-start(bf16[128,512]{1,0:T(8,128)(2,1)S(1)} %fusion.56), channel_id=1, source_target_pairs={{0,32},{4,36},{8,40},{12,44},{16,48},{20,52},{24,56},{28,60},{32,0... | collective-permute-start | bytes 393224 | tf_op jit(solution)/shard_map/ppermute | solution.py:15
  109.6 6.3 %copy-start.29 = (f32[512,4]{0,1:T(4,128)S(1)}, f32[512,4]{0,1:T(4,128)}, u32[]{:S(2)}) copy-start(f32[512,4]{0,1:T(4,128)} %get-tuple-element.14) | copy-start | bytes 24580
  109.6 7.2 %copy-start.28 = (f32[512,4]{0,1:T(4,128)S(1)}, f32[512,4]{0,1:T(4,128)}, u32[]{:S(2)}) copy-start(f32[512,4]{0,1:T(4,128)} %get-tuple-element.15) | copy-start | bytes 24580
  170.9 2.4 %copy-start.9 = (f32[512,4]{1,0:T(8,128)S(1)}, f32[512,4]{1,0:T(8,128)}, u32[]{:S(2)}) copy-start(f32[512,4]{1,0:T(8,128)} %copy.326) | copy-start | bytes 24580
  171.1 2.8 %copy-start.8 = (f32[512,4]{1,0:T(8,128)S(1)}, f32[512,4]{1,0:T(8,128)}, u32[]{:S(2)}) copy-start(f32[512,4]{1,0:T(8,128)} %copy.314) | copy-start | bytes 24580
  (10 other events, 16.5 us)
Sparse Core Ops, SparseCore 0:
  10.5 160.4 all-gather.1
  183.5 33.1 reduce-scatter.1
where the time goes:
time: 224 us; the launch traced here: 223 us
  waiting for transfers between devices  102 us (46%)
  local copies, waits for them, and re-layouts  52.1 us (23%)
  starting transfers between devices  31.7 us (14%)
  between operations  14.6 us (7%)
  other arithmetic  14.2 us (6%)
  matrix products  8.56 us (4%)
    all_gather x1, waiting for transfers between devices, body(): lax.all_gather(out_weight, 'seq', axis=1, tiled=True)  53.3 us
    reduce_scatter x1, waiting for transfers between devices, body(): lax.psum_scatter(rounded_terms.astype(jnp.bfloat16), 'head', scatter_dime...  33.3 us
    ppermute x8, starting transfers between devices, partner(): return lax.ppermute(value, axis, pairs)  31.6 us
    ppermute x8, waiting for transfers between devices, partner(): return lax.ppermute(value, axis, pairs)  15 us
    exp x5, local copies, waits for them, and re-layouts, merge_level(): keep_old = jnp.exp(running_max - newest)  6.4 us
    ppermute x8, local copies, waits for them, and re-layouts, partner(): return lax.ppermute(value, axis, pairs)  6.36 us
  transfers between devices with their start and end apart: 10, of which 5 were waited for; matrix products, arithmetic and copies ran while one was open for 28% of the time, Pallas kernels for 0%

commit v1 on v0

--- a/solution.py
+++ b/solution.py
@@ -148,7 +148,7 @@
     )
     partial_terms = jnp.dot(
         attended,
-        lax.all_gather(out_weight, "seq", axis=1, tiled=True),
+        jnp.concatenate(lax.all_gather(out_weight, "seq"), axis=1),
         preferred_element_type=jnp.float32,
     )
     rounded_terms = partial_terms.astype(jnp.bfloat16).astype(jnp.float32)

time: 224 us -> 220 us (0.982)
  local copies, waits for them, and re-layouts: 52.1 us -> 32.7 us
  waiting for transfers between devices: 102 us -> 119 us
    all_gather x1, waiting for transfers between devices: 53.3 us -> 66.1 us  [body(): lax.all_gather(out_weight, 'seq')]
    exp x10 -> x0, local copies, waits for them, and re-layouts: 7.84 us -> none  [the longest x5 6.4 us: merge_level(): keep_old = jnp.exp(running_max - newest)]
    mul x10 -> x0, local copies, waits for them, and re-layouts: 7.01 us -> none  [the longest x5 3.99 us: merge_level(): running_out * keep_old[..., None] + weighted_value_sum * keep_new[..., None]]
    ppermute x8, waiting for transfers between devices: 15 us -> 19.7 us  [partner(): return lax.ppermute(value, axis, pairs)]
    convert_element_type x0 -> x1, other arithmetic: none -> 3.77 us  [body(): (running[2] / running[1][..., None]).reshape(row_count, col_count)]
    ppermute x8, local copies, waits for them, and re-layouts: 6.36 us -> 3.65 us  [partner(): return lax.ppermute(value, axis, pairs)]
  transfers between devices with their start and end apart: 10 -> 10, of which waited for: 5 -> 5; matrix products, arithmetic and copies ran while one was open for 28% -> 20% of each run, Pallas kernels for 0% -> 0%
where the time goes in v1:
time: 220 us; the launch traced here: 219 us
  waiting for transfers between devices  119 us (54%)
  local copies, waits for them, and re-layouts  32.7 us (15%)
  starting transfers between devices  31.5 us (14%)
  between operations  14.4 us (7%)
  other arithmetic  12.9 us (6%)
  matrix products  9.13 us (4%)
    all_gather x1, waiting for transfers between devices, body(): lax.all_gather(out_weight, 'seq')  66.1 us
    reduce_scatter x1, waiting for transfers between devices, body(): lax.psum_scatter(rounded_terms.astype(jnp.bfloat16), 'head', scatter_dime...  32.8 us
    ppermute x8, starting transfers between devices, partner(): return lax.ppermute(value, axis, pairs)  31.3 us
    ppermute x8, waiting for transfers between devices, partner(): return lax.ppermute(value, axis, pairs)  19.7 us
    dot_general x6, matrix products, level_terms(): jnp.einsum('bqhd,bkhd->bhqk', blocked_query_rows, blocked_key_rows, prefe...  4.7 us
  transfers between devices with their start and end apart: 10, of which 5 were waited for; matrix products, arithmetic and copies ran while one was open for 20% of the time, Pallas kernels for 0%

profile of v1, /device:TPU:1, one launch (start us, length us, event | category | flops | bytes accessed | tf_op | source)
XLA Modules:
  0.0 219.4 jit_solution(11495291317112412173)
XLA Ops:
  6.5 1.7 reshape.872
  10.0 8.7 %collective-permute-start = (bf16[128,512]{1,0:T(8,128)(2,1)S(1)}, bf16[128,512]{1,0:T(8,128)(2,1)}, u32[]{:S(2)}, u32[]{:S(2)}) collective-permute-start(bf16[128,512]{1,0:T(8,128)(2,1)S(1)} %fusion.57), channel_id=1, source_target_pairs={{0,4},{4,0},{8,12},{12,8},{16,20},{20,16},{24,28},{28,24},{32,36},... | collective-permute-start | bytes 393224 | tf_op jit(solution)/shard_map/ppermute | solution.py:15
  21.8 1.9 collective-permute-start.1
  26.3 1.1 reshape.875
  27.6 0.9 reshape_reshape.9
  28.6 0.9 reshape.817
  31.2 1.1 convert_reduce_fusion.1
  32.8 1.4 convert_reduce_fusion.3
  35.1 0.8 rev.13
  35.9 0.9 copy.231
  37.9 1.8 bitcast_reduce_fusion
  39.7 1.0 fusion.1
  44.0 1.1 broadcast_select_fusion.9
  45.9 1.9 collective-permute-start.2
  48.7 3.4 %collective-permute-start.3 = (bf16[128,512]{1,0:T(8,128)(2,1)S(1)}, bf16[128,512]{1,0:T(8,128)(2,1)S(1)}, u32[]{:S(2)}, u32[]{:S(2)}) collective-permute-start(bf16[128,512]{1,0:T(8,128)(2,1)S(1)} %fusion.55), channel_id=1, source_target_pairs={{0,8},{4,12},{8,0},{12,4},{16,24},{20,28},{24,16},{28,20},{32,40},... | collective-permute-start | bytes 393224 | tf_op jit(solution)/shard_map/ppermute | solution.py:15
  52.1 1.0 copy.254
  55.2 1.0 copy.259
  57.5 2.1 collective-permute-start.5
  60.5 4.3 %collective-permute-start.4 = (bf16[128,512]{1,0:T(8,128)(2,1)S(1)}, bf16[128,512]{1,0:T(8,128)(2,1)S(1)}, u32[]{:S(2)}, u32[]{:S(2)}) collective-permute-start(bf16[128,512]{1,0:T(8,128)(2,1)S(1)} %fusion.59), channel_id=1, source_target_pairs={{0,16},{4,20},{8,24},{12,28},{16,0},{20,4},{24,8},{28,12},{32,48},... | collective-permute-start | bytes 393224 | tf_op jit(solution)/shard_map/ppermute | solution.py:15
  64.9 1.1 fusion.121
  68.2 2.8 %collective-permute-done.5 = bf16[128,512]{1,0:T(8,128)(2,1)S(1)} collective-permute-done((bf16[128,512]{1,0:T(8,128)(2,1)S(1)}, bf16[128,512]{1,0:T(8,128)(2,1)S(1)}, u32[]{:S(2)}, u32[]{:S(2)}) %collective-permute-start.5) | collective-permute-done | bytes 131104 | tf_op jit(solution)/shard_map/ppermute | solution.py:15
  71.7 1.9 collective-permute-start.7
  74.8 7.1 %collective-permute-start.6 = (bf16[128,512]{1,0:T(8,128)(2,1)S(1)}, bf16[128,512]{1,0:T(8,128)(2,1)S(1)}, u32[]{:S(2)}, u32[]{:S(2)}) collective-permute-start(bf16[128,512]{1,0:T(8,128)(2,1)S(1)} %fusion.60), channel_id=1, source_target_pairs={{0,32},{4,36},{8,40},{12,44},{16,48},{20,52},{24,56},{28,60},{32,0... | collective-permute-start | bytes 393224 | tf_op jit(solution)/shard_map/ppermute | solution.py:15
  82.0 1.0 fusion.120
  83.9 16.7 %collective-permute-done.6 = bf16[128,512]{1,0:T(8,128)(2,1)S(1)} collective-permute-done((bf16[128,512]{1,0:T(8,128)(2,1)S(1)}, bf16[128,512]{1,0:T(8,128)(2,1)S(1)}, u32[]{:S(2)}, u32[]{:S(2)}) %collective-permute-start.6) | collective-permute-done | bytes 131104 | tf_op jit(solution)/shard_map/ppermute | solution.py:15
  101.5 1.0 copy.285
  103.5 3.8 %fusion.13 = bf16[512,4,128]{2,0,1:T(8,128)(2,1)S(1)} fusion(f32[4,128,4,128]{3,1,0,2:T(8,128)S(1)} %copy.234, f32[512,4,128]{2,0,1:T(8,128)S(1)} %bitcast.280, f32[512,4,128]{2,0,1:T(8,128)S(1)} %bitcast.281, f32[512,4]{0,1:T(4,128)S(1)} %get-tuple-element.5, f32[512,4]{0,1:T(4,128)S(1)} %get-tuple-element.10, ...), kind=kLoop, calls=%fused_computation.27 | loop fusion | flops 4456448 | bytes 3989504 | tf_op jit(solution)/shard_map/convert_element_type | solution.py:147
  107.5 66.1 %all-gather.3.cloned.1.call-done = bf16[65536,16]{0,1:T(8,128)(2,1)} async-done(((bf16[512,16]{0,1:T(8,128)(2,1)}), bf16[65536,16]{0,1:T(8,128)(2,1)}) %all-gather.3.cloned.1.call-update) | async-done | bytes 2097168 | tf_op jit(solution)/shard_map/all_gather | solution.py:151
  173.6 2.3 %copy.330 = bf16[2,8,128,512]{3,2,1,0:T(8,128)(2,1)S(1)} copy(bf16[2,8,128,512]{3,1,2,0:T(8,128)(2,1)} %bitcast.283) | data formatting | bytes 4194304
  175.8 1.2 copy.290
  177.0 2.7 %convolution_convert_fusion = bf16[512,2048]{1,0:T(8,128)(2,1)} fusion(bf16[512,512]{0,1:T(8,128)(2,1)S(1)} %bitcast.292, bf16[512,2048]{0,1:T(8,128)(2,1)S(1)} %bitcast.284), kind=kOutput, calls=%fused_computation | convolution fusion | flops 1074790400 | bytes 4718592 | tf_op jit(solution)/shard_map/dot_general | solution.py:149
  179.7 32.8 %reduce-scatter.2.cloned.1.call-done = bf16[512,512]{1,0:T(8,128)(2,1)} async-done(((bf16[512,2048]{1,0:T(8,128)(2,1)}), bf16[512,512]{1,0:T(8,128)(2,1)}) %reduce-scatter.2.cloned.1.call-update) | async-done | bytes 524304 | tf_op jit(solution)/shard_map/reduce_scatter | solution.py:155
  (167 shorter events, 27.4 us)
Async XLA Ops:
  6.5 167.0 %all-gather.3.cloned.1.call-start = ((), (), s32[]{:S(2)}) async-start(), calls=%async_computation.2 | async-start | bytes 2113536 | tf_op jit(solution)/shard_map/all_gather | solution.py:151
  9.1 9.7 %copy-start.1 = (bf16[512,512]{1,0:T(8,128)(2,1)S(1)}, bf16[512,512]{1,0:T(8,128)(2,1)}, u32[]{:S(2)}) copy-start(bf16[512,512]{1,0:T(8,128)(2,1)} %param.6) | copy-start | bytes 1572868
  10.0 34.1 %collective-permute-start = (bf16[128,512]{1,0:T(8,128)(2,1)S(1)}, bf16[128,512]{1,0:T(8,128)(2,1)}, u32[]{:S(2)}, u32[]{:S(2)}) collective-permute-start(bf16[128,512]{1,0:T(8,128)(2,1)S(1)} %fusion.57), channel_id=1, source_target_pairs={{0,4},{4,0},{8,12},{12,8},{16,20},{20,16},{24,28},{28,24},{32,36},... | collective-permute-start | bytes 393224 | tf_op jit(solution)/shard_map/ppermute | solution.py:15
  20.2 4.5 %copy-start.2 = (bf16[512,512]{1,0:T(8,128)(2,1)S(1)}, bf16[512,512]{1,0:T(8,128)(2,1)}, u32[]{:S(2)}) copy-start(bf16[512,512]{1,0:T(8,128)(2,1)} %param.4) | copy-start | bytes 1572868
  21.8 22.2 %collective-permute-start.1 = (bf16[128,512]{1,0:T(8,128)(2,1)}, bf16[128,512]{1,0:T(8,128)(2,1)}, u32[]{:S(2)}, u32[]{:S(2)}) collective-permute-start(bf16[128,512]{1,0:T(8,128)(2,1)} %fusion.54), channel_id=1, source_target_pairs={{0,4},{4,0},{8,12},{12,8},{16,20},{20,16},{24,28},{28,24},{32,36},... | collective-permute-start | bytes 393224 | tf_op jit(solution)/shard_map/ppermute | solution.py:15
  23.7 188.8 %reduce-scatter.2.cloned.1.call-start = ((), (), s32[]{:S(2)}) async-start(), calls=%async_computation.1 | async-start | bytes 2621440 | tf_op jit(solution)/shard_map/reduce_scatter | solution.py:155
  25.4 2.2 copy-start
  28.6 2.0 copy-start.4
  30.6 3.6 %copy-start.5 = (bf16[1,2,128,4,128]{4,3,2,1,0:T(4,128)(2,1)S(1)}, bf16[1,2,128,4,128]{4,3,2,1,0:T(4,128)(2,1)}, u32[]{:S(2)}) copy-start(bf16[1,2,128,4,128]{4,3,2,1,0:T(4,128)(2,1)} %convert_element_type.255) | copy-start | bytes 786436
  30.6 4.3 %copy-start.3 = (bf16[2,2,128,4,128]{4,3,2,1,0:T(4,128)(2,1)S(1)}, bf16[2,2,128,4,128]{4,3,2,1,0:T(4,128)(2,1)}, u32[]{:S(2)}) copy-start(bf16[2,2,128,4,128]{4,3,2,1,0:T(4,128)(2,1)} %reshape_reshape.9) | copy-start | bytes 1572868
  35.0 1.8 copy-start.7
  35.0 2.2 copy-start.6
  40.7 0.8 copy-start.8
  45.9 13.7 %collective-permute-start.2 = (bf16[128,512]{1,0:T(8,128)(2,1)S(1)}, bf16[128,512]{1,0:T(8,128)(2,1)S(1)}, u32[]{:S(2)}, u32[]{:S(2)}) collective-permute-start(bf16[128,512]{1,0:T(8,128)(2,1)S(1)} %fusion.58), channel_id=1, source_target_pairs={{0,8},{4,12},{8,0},{12,4},{16,24},{20,28},{24,16},{28,20},{32,40},... | collective-permute-start | bytes 393224 | tf_op jit(solution)/shard_map/ppermute | solution.py:15
  48.7 7.9 %collective-permute-start.3 = (bf16[128,512]{1,0:T(8,128)(2,1)S(1)}, bf16[128,512]{1,0:T(8,128)(2,1)S(1)}, u32[]{:S(2)}, u32[]{:S(2)}) collective-permute-start(bf16[128,512]{1,0:T(8,128)(2,1)S(1)} %fusion.55), channel_id=1, source_target_pairs={{0,8},{4,12},{8,0},{12,4},{16,24},{20,28},{24,16},{28,20},{32,40},... | collective-permute-start | bytes 393224 | tf_op jit(solution)/shard_map/ppermute | solution.py:15
  57.5 13.5 %collective-permute-start.5 = (bf16[128,512]{1,0:T(8,128)(2,1)S(1)}, bf16[128,512]{1,0:T(8,128)(2,1)S(1)}, u32[]{:S(2)}, u32[]{:S(2)}) collective-permute-start(bf16[128,512]{1,0:T(8,128)(2,1)S(1)} %fusion.56), channel_id=1, source_target_pairs={{0,16},{4,20},{8,24},{12,28},{16,0},{20,4},{24,8},{28,12},{32,48},... | collective-permute-start | bytes 393224 | tf_op jit(solution)/shard_map/ppermute | solution.py:15
  60.0 7.6 %copy-start.9 = (f32[512,4]{0,1:T(4,128)S(1)}, f32[512,4]{0,1:T(4,128)}, u32[]{:S(2)}) copy-start(f32[512,4]{0,1:T(4,128)} %reshape.834) | copy-start | bytes 24580
  60.5 13.4 %collective-permute-start.4 = (bf16[128,512]{1,0:T(8,128)(2,1)S(1)}, bf16[128,512]{1,0:T(8,128)(2,1)S(1)}, u32[]{:S(2)}, u32[]{:S(2)}) collective-permute-start(bf16[128,512]{1,0:T(8,128)(2,1)S(1)} %fusion.59), channel_id=1, source_target_pairs={{0,16},{4,20},{8,24},{12,28},{16,0},{20,4},{24,8},{28,12},{32,48},... | collective-permute-start | bytes 393224 | tf_op jit(solution)/shard_map/ppermute | solution.py:15
  67.2 4.2 %copy-start.11 = (f32[512,4]{0,1:T(4,128)}, f32[512,4]{0,1:T(4,128)S(1)}, u32[]{:S(2)}) copy-start(f32[512,4]{0,1:T(4,128)S(1)} %reshape.840) | copy-start | bytes 24580
  71.7 29.8 %collective-permute-start.7 = (bf16[128,512]{1,0:T(8,128)(2,1)S(1)}, bf16[128,512]{1,0:T(8,128)(2,1)}, u32[]{:S(2)}, u32[]{:S(2)}) collective-permute-start(bf16[128,512]{1,0:T(8,128)(2,1)S(1)} %bitcast.299), channel_id=1, source_target_pairs={{0,32},{4,36},{8,40},{12,44},{16,48},{20,52},{24,56},{28,60},{32,0... | collective-permute-start | bytes 393224 | tf_op jit(solution)/shard_map/ppermute | solution.py:15
  74.0 26.8 %copy-start.13 = (bf16[16,512]{1,0:T(8,128)(2,1)S(1)}, bf16[16,512]{1,0:T(8,128)(2,1)}, u32[]{:S(2)}) copy-start(bf16[16,512]{1,0:T(8,128)(2,1)} %convert_reduce_fusion.4) | copy-start | bytes 49156
  74.3 28.5 %copy-start.10 = (f32[512,4]{0,1:T(4,128)S(1)}, f32[512,4]{0,1:T(4,128)}, u32[]{:S(2)}) copy-start(f32[512,4]{0,1:T(4,128)} %reshape.834) | copy-start | bytes 24580
  74.3 28.5 %copy-start.12 = (f32[512,4]{0,1:T(4,128)S(1)}, f32[512,4]{0,1:T(4,128)}, u32[]{:S(2)}) copy-start(f32[512,4]{0,1:T(4,128)} %copy-done.11) | copy-start | bytes 24580
  74.3 28.5 %copy-start.14 = (f32[4,4,128]{2,1,0:T(4,128)S(1)}, f32[4,4,128]{2,1,0:T(4,128)}, u32[]{:S(2)}) copy-start(f32[4,4,128]{2,1,0:T(4,128)} %fusion.1) | copy-start | bytes 24580
  74.3 28.5 %copy-start.15 = (f32[512,4]{0,1:T(4,128)S(1)}, f32[512,4]{0,1:T(4,128)}, u32[]{:S(2)}) copy-start(f32[512,4]{0,1:T(4,128)} %copy.288) | copy-start | bytes 24580
  74.3 28.5 %copy-start.16 = (f32[512,4]{0,1:T(4,128)S(1)}, f32[512,4]{0,1:T(4,128)}, u32[]{:S(2)}) copy-start(f32[512,4]{0,1:T(4,128)} %reshape.860) | copy-start | bytes 24580
  74.4 28.5 %copy-start.17 = (f32[512,4]{0,1:T(4,128)S(1)}, f32[512,4]{0,1:T(4,128)}, u32[]{:S(2)}) copy-start(f32[512,4]{0,1:T(4,128)} %reshape.862) | copy-start | bytes 24580
  74.4 28.5 %copy-start.18 = (f32[512,4]{0,1:T(4,128)S(1)}, f32[512,4]{0,1:T(4,128)}, u32[]{:S(2)}) copy-start(f32[512,4]{0,1:T(4,128)} %get-tuple-element.18) | copy-start | bytes 24580
  74.4 28.5 %copy-start.19 = (f32[512,4]{0,1:T(4,128)S(1)}, f32[512,4]{0,1:T(4,128)}, u32[]{:S(2)}) copy-start(f32[512,4]{0,1:T(4,128)} %get-tuple-element.19) | copy-start | bytes 24580
  74.8 25.8 %collective-permute-start.6 = (bf16[128,512]{1,0:T(8,128)(2,1)S(1)}, bf16[128,512]{1,0:T(8,128)(2,1)S(1)}, u32[]{:S(2)}, u32[]{:S(2)}) collective-permute-start(bf16[128,512]{1,0:T(8,128)(2,1)S(1)} %fusion.60), channel_id=1, source_target_pairs={{0,32},{4,36},{8,40},{12,44},{16,48},{20,52},{24,56},{28,60},{32,0... | collective-permute-start | bytes 393224 | tf_op jit(solution)/shard_map/ppermute | solution.py:15
Sparse Core Ops, SparseCore 0:
  23.9 149.6 all-gather.2
  179.8 32.6 reduce-scatter.1
